TPU v7x, 32 devices: a whole 2x2x4 slice. The times are simulated.
32 devices in a mesh: tbl: 8 (over z, y), pair: 4 (over x, core).
Axes of the slice: x: 2, y: 2, z: 4, core: 2. Of those that a mesh axis runs over, the one named last changes fastest.
Arguments:
- codes: bfloat16 [112, 64, 16384], P('tbl', None, 'pair'), may hold values from -127 to 127
- scales: float32 [112, 16384], P('tbl', 'pair'), may hold values from 0.002 to 0.02
- shard_slot: int32 [8, 14], replicated, may hold values from -1 to 53, as said below
- weight_first: bfloat16 [351, 1024], replicated, may hold values from -0.3125 to 0.3125
- bias_first: float32 [1024], replicated, may hold values from -3 to 3
- weight_second: bfloat16 [1024, 1024], replicated, may hold values from -0.1875 to 0.1875
- bias_second: float32 [1024], replicated, may hold values from -3 to 3
- weight_third: bfloat16 [1024, 512], replicated, may hold values from -0.1875 to 0.1875
- bias_third: float32 [512], replicated, may hold values from -3 to 3
- weight_fourth: bfloat16 [512, 256], replicated, may hold values from -0.25 to 0.25
- bias_fourth: float32 [256], replicated, may hold values from -3 to 3
- weight_out: bfloat16 [256], replicated, may hold values from -0.375 to 0.375
- bias_out: float32 [1], replicated, may hold values from -3 to 3
Outputs:
- logits: float32 [4, 4096], P(None, 'tbl')
Inputs may be any that keep to these rules, and one draw needn't show every extreme that they name: `shard_slot`: each shard 0 to 53 stands in exactly one slot; all other slots hold -1. For k below half of the tbl size, row k holds its shards in its first slots and the row half the tbl size further holds its shards in its last slots, and the two rows hold 14 shards or fewer together. Some row holds 14 shards.
All inputs are finite; a program needn't handle non-finite values.
Results may differ from a plain program's by a relative error of at most 0.03.
Values may be sent and summed in bfloat16 or wider, within the bound.
No kernel may reach another device: no remote copies, remote signals or barrier semaphores. Data moves between devices by JAX's collectives and lax.ppermute only.
A program may use at most 128 MiB of HBM per device.

v0:
```python
import jax
import jax.numpy as jnp
import numpy as np
from jax import lax
from jax.sharding import PartitionSpec as P

TABLES = 27


def pair_columns(tables):
    first, second = np.triu_indices(tables, 1)
    return (first * tables + second).astype(np.int32)


def shard_positions(slot_table, shard_total):
    flat = slot_table.reshape(-1)
    matches = flat[None, :] == jnp.arange(shard_total, dtype=jnp.int32)[:, None]
    places = jnp.arange(flat.shape[0], dtype=jnp.int32)[None, :]
    return jnp.sum(jnp.where(matches, places, 0), axis=1)


def dense_layer(inputs, weight, bias):
    product = jnp.dot(
        inputs.astype(jnp.float32), weight.astype(jnp.float32), precision=lax.Precision.HIGHEST
    )
    return jax.nn.relu(product + bias).astype(jnp.bfloat16)


def score_samples(picked_codes, picked_scales, layers):
    table_count = picked_codes.shape[0] // 2
    column_count = picked_codes.shape[1]
    count = picked_codes.shape[2]
    halves = picked_codes.reshape(table_count, 2, column_count, count)
    half_scales = picked_scales.reshape(table_count, 2, count)
    gram = jnp.zeros((count, table_count, table_count), jnp.float32)
    for part_index in range(2):
        block_codes = halves[:, part_index].astype(jnp.float32)
        products = jnp.einsum(
            "icb,jcb->bij", block_codes, block_codes, precision=lax.Precision.HIGHEST
        )
        factor = half_scales[:, part_index]
        outer = jnp.transpose(factor)[:, :, None] * jnp.transpose(factor)[:, None, :]
        gram = gram + products * outer
    flat = gram.reshape(count, table_count * table_count)
    hidden = flat[:, pair_columns(table_count)].astype(jnp.bfloat16)
    for weight, bias in layers[:-1]:
        hidden = dense_layer(hidden, weight, bias)
    weight_last, bias_last = layers[-1]
    final = jnp.dot(
        hidden.astype(jnp.float32), weight_last.astype(jnp.float32), precision=lax.Precision.HIGHEST
    )
    return final + bias_last[0]


def per_device(
    codes,
    scales,
    shard_slot,
    weight_first,
    bias_first,
    weight_second,
    bias_second,
    weight_third,
    bias_third,
    weight_fourth,
    bias_fourth,
    weight_out,
    bias_out,
):
    layers = (
        (weight_first, bias_first),
        (weight_second, bias_second),
        (weight_third, bias_third),
        (weight_fourth, bias_fourth),
        (weight_out, bias_out),
    )
    slot_count = codes.shape[0]
    column_count = codes.shape[1]
    tbl_count = lax.axis_size("tbl")
    batch_local = codes.shape[2] // tbl_count
    shard_total = 2 * TABLES

    def make_scorer(positions):

        def scorer(received):
            got_codes, got_scales = received
            picked_codes = jnp.take(got_codes[:, :, 0, :], positions, axis=0)
            picked_scales = jnp.take(got_scales[:, 0, 0, :], positions, axis=0)
            return score_samples(picked_codes, picked_scales, layers)

        return scorer

    packed_codes = codes.reshape(slot_count, column_count, tbl_count, batch_local)
    packed_scales = scales.reshape(slot_count, 1, tbl_count, batch_local)
    scorer = make_scorer(shard_positions(shard_slot, shard_total))
    logits = scorer(
        (
            lax.all_to_all(packed_codes, "tbl", split_axis=2, concat_axis=0, tiled=True),
            lax.all_to_all(
                packed_scales.astype(jnp.bfloat16), "tbl", split_axis=2, concat_axis=0, tiled=True
            ).astype(packed_scales.dtype),
        )
    )
    return lax.all_gather(logits[None, :], "pair", axis=0, tiled=True)


def solution(mesh):
    return jax.shard_map(
        per_device,
        mesh=mesh,
        in_specs=(
            P("tbl", None, "pair"),
            P("tbl", "pair"),
            P(),
            P(),
            P(),
            P(),
            P(),
            P(),
            P(),
            P(),
            P(),
            P(),
            P(),
        ),
        out_specs=P(None, "tbl"),
        check_vma=False,
    )
```

profile of v0, /device:TPU:0, one launch (start us, length us, event | category | flops | bytes accessed | tf_op | source)
XLA Modules:
  0.0 243.0 jit_solution(14735998043598674516)
XLA Ops:
  0.0 0.0 copy-start
  0.0 1.1 convert_element_type.56
  1.2 0.7 copy.51
  1.9 7.3 %all-to-all-start.1 = ((bf16[14,1,8,512]{3,0,1,2:T(8,128)(2,1)}), bf16[14,1,8,512]{3,0,1,2:T(8,128)(2,1)S(1)}, u32[]{:S(2)}, u32[]{:S(2)}) async-start(bf16[14,1,8,512]{3,0,1,2:T(8,128)(2,1)} %copy.51), calls=%async_computation.1 | async-start | bytes 262144 | tf_op jit(solution)/shard_map/all_to_all | solution.py:99
  9.2 7.2 %copy.60 = bf16[14,8,8,8,512]{4,3,1,0,2:T(8,128)(2,1)} copy(bf16[14,8,8,8,512]{4,3,2,1,0:T(8,128)(2,1)} %bitcast.62) | data formatting | bytes 14680064 | tf_op jit(solution)/shard_map/reshape | solution.py:93
  16.4 0.1 all-to-all-done.1
  16.5 0.0 copy-start.2
  16.5 0.0 copy-start.10
  16.5 0.0 copy-start.3
  16.5 6.0 %all-to-all-start = ((bf16[14,64,8,512]{3,1,0,2:T(8,128)(2,1)}), bf16[14,64,8,512]{3,1,0,2:T(8,128)(2,1)}, u32[]{:S(2)}, u32[]{:S(2)}) async-start(bf16[14,64,8,512]{3,1,0,2:T(8,128)(2,1)} %bitcast.60), calls=%async_computation | async-start | bytes 14680064 | tf_op jit(solution)/shard_map/all_to_all | solution.py:98
  22.6 0.0 copy-done.2
  22.6 0.1 eq.15
  22.6 0.1 select_reduce_fusion
  22.8 0.1 reduce_sum.14
  22.9 0.1 copy.47
  23.0 0.0 copy-done.10
  23.7 0.0 copy-done.3
  23.8 0.6 gather_fusion.1
  24.4 0.1 gather.18
  24.5 0.2 copy.52
  24.8 157.9 %all-to-all-done = bf16[14,64,8,512]{3,1,0,2:T(8,128)(2,1)} async-done(((bf16[14,64,8,512]{3,1,0,2:T(8,128)(2,1)}), bf16[14,64,8,512]{3,1,0,2:T(8,128)(2,1)}, u32[]{:S(2)}, u32[]{:S(2)}) %all-to-all-start) | async-done | bytes 7340064 | tf_op jit(solution)/shard_map/all_to_all | solution.py:98
  182.7 5.7 %gather_fusion = bf16[54,64,512]{2,1,0:T(8,128)(2,1)} fusion(bf16[112,64,512]{2,1,0:T(8,128)(2,1)} %bitcast.2, s32[1024]{0:T(1024)S(1)} %pad_clamp_fusion.1), kind=kCustom, calls=%fused_computation | custom fusion | bytes 7078104 | tf_op jit(solution)/shard_map/jit(_take)/gather | solution.py:87
  188.4 13.0 %copy.49 = bf16[27,2,64,512]{2,0,3,1:T(8,128)(2,1)} copy(bf16[27,2,64,512]{3,2,1,0:T(8,128)(2,1)} %bitcast.61) | data formatting | bytes 7077888 | tf_op jit(solution)/shard_map/jit(_take)/gather | solution.py:87
  201.5 7.4 %broadcast_select_fusion = bf16[27,2,64,512]{2,0,3,1:T(8,128)(2,1)} fusion(bf16[27,2,64,512]{2,0,3,1:T(8,128)(2,1)} %copy.49, pred[27,2]{0,1:T(4,128)(4,1)S(1)} %copy.47), kind=kLoop, calls=%fused_computation.4 | loop fusion | flops 1769472 | bytes 7077942 | tf_op jit(solution)/shard_map/jit(_take)/select_n | solution.py:87
  208.9 5.9 %fusion = f32[512,27,27]{2,1,0:T(8,128)S(1)} fusion(bf16[27,2,64,512]{2,0,3,1:T(8,128)(2,1)} %broadcast_select_fusion), kind=kOutput, calls=%fused_computation.7 | convolution fusion | flops 47775744 | bytes 5687296 | tf_op jit(solution)/shard_map/icb,jcb->bij/dot_general | solution.py:38
  214.7 0.0 copy-done.1
  214.7 6.7 %multiply_add_fusion = bf16[512,27,27]{2,1,0:T(8,128)(2,1)} fusion(f32[512,27,27]{2,1,0:T(8,128)S(1)} %fusion, f32[512,27]{1,0:T(8,128)S(1)} %get-tuple-element.6, f32[512,27]{1,0:T(8,128)S(1)} %get-tuple-element.5, bf16[27,2,64,512]{2,0,3,1:T(8,128)(2,1)S(1)} %copy-done.1), kind=kOutput, calls=%fused_computation.3 | convolution fusion | flops 50015232 | bytes 14377984 | tf_op jit(solution)/shard_map/icb,jcb->bij/dot_general | solution.py:38
  221.5 7.7 %reshape.100 = bf16[512,729]{1,0:T(8,128)(2,1)} reshape(bf16[512,27,27]{2,1,0:T(8,128)(2,1)} %multiply_add_fusion) | data formatting | bytes 1492992 | tf_op jit(solution)/shard_map/reshape | solution.py:44
  229.2 1.4 copy.54
  230.6 0.0 copy-start.8
  230.6 2.0 gather_fusion.2
  232.7 0.0 copy-done.6
  232.7 0.0 copy-start.4
  232.7 0.0 copy-start.5
  232.7 0.0 copy-start.9
  232.7 1.9 maximum_convert_fusion.1
  234.7 0.0 copy-done
  234.7 0.0 copy-done.7
  234.7 1.3 maximum_convert_fusion
  236.0 0.0 copy-done.8
  236.0 0.0 copy-done.4
  236.0 0.7 fusion.3
  236.7 0.0 copy-done.5
  236.7 0.0 copy-done.9
  236.7 0.3 fusion.5
  237.0 0.2 fusion.8
  237.2 5.2 %all-gather.1 = f32[4,1,512]{2,1,0:T(1,128)S(1)} all-gather(f32[1,1,512]{2,1,0:T(1,128)S(1)} %bitcast.66), channel_id=2, replica_groups=mesh['tbl'=8,'pair'=4] {'pair'}, dimensions={0}, use_global_device_ids=true | all-gather | bytes 10240 | tf_op jit(solution)/shard_map/all_gather | solution.py:104
  242.4 0.6 copy.61
  (15 shorter events, 0.2 us)
Async XLA Ops:
  0.0 234.7 %copy-start = (bf16[1024,1024]{1,0:T(8,128)(2,1)S(1)}, bf16[1024,1024]{1,0:T(8,128)(2,1)}, u32[]{:S(2)}) copy-start(bf16[1024,1024]{1,0:T(8,128)(2,1)} %param.20) | copy-start | bytes 6291460
  1.9 14.7 %all-to-all-start.1 = ((bf16[14,1,8,512]{3,0,1,2:T(8,128)(2,1)}), bf16[14,1,8,512]{3,0,1,2:T(8,128)(2,1)S(1)}, u32[]{:S(2)}, u32[]{:S(2)}) async-start(bf16[14,1,8,512]{3,0,1,2:T(8,128)(2,1)} %copy.51), calls=%async_computation.1 | async-start | bytes 262144 | tf_op jit(solution)/shard_map/all_to_all | solution.py:99
  16.5 6.0 %copy-start.2 = (s32[8,14]{1,0:T(8,128)S(1)}, s32[8,14]{1,0:T(8,128)}, u32[]{:S(2)}) copy-start(s32[8,14]{1,0:T(8,128)} %param.17) | copy-start | bytes 1348
  16.5 6.5 %copy-start.10 = (bf16[256]{0:T(256)(128)(2,1)S(1)}, bf16[256]{0:T(256)(128)(2,1)}, u32[]{:S(2)}) copy-start(bf16[256]{0:T(256)(128)(2,1)} %param.26) | copy-start | bytes 1540
  16.5 7.1 %copy-start.3 = (s32[351]{0:T(512)S(1)}, s32[351]{0:T(512)}, u32[]{:S(2)}) copy-start(s32[351]{0:T(512)} %constant.49) | copy-start | bytes 4216
  16.5 166.2 %all-to-all-start = ((bf16[14,64,8,512]{3,1,0,2:T(8,128)(2,1)}), bf16[14,64,8,512]{3,1,0,2:T(8,128)(2,1)}, u32[]{:S(2)}, u32[]{:S(2)}) async-start(bf16[14,64,8,512]{3,1,0,2:T(8,128)(2,1)} %bitcast.60), calls=%async_computation | async-start | bytes 14680064 | tf_op jit(solution)/shard_map/all_to_all | solution.py:98
  208.9 5.9 %copy-start.1 = (bf16[27,2,64,512]{2,0,3,1:T(8,128)(2,1)S(1)}, bf16[27,2,64,512]{2,0,3,1:T(8,128)(2,1)}, u32[]{:S(2)}) copy-start(bf16[27,2,64,512]{2,0,3,1:T(8,128)(2,1)} %broadcast_select_fusion) | copy-start | bytes 10616836
  221.5 11.2 %copy-start.6 = (f32[1024]{0:T(1024)S(1)}, f32[1024]{0:T(1024)}, u32[]{:S(2)}) copy-start(f32[1024]{0:T(1024)} %param.19) | copy-start | bytes 12292
  221.5 13.2 %copy-start.7 = (f32[1024]{0:T(1024)S(1)}, f32[1024]{0:T(1024)}, u32[]{:S(2)}) copy-start(f32[1024]{0:T(1024)} %param.21) | copy-start | bytes 12292
  230.6 5.4 %copy-start.8 = (f32[512]{0:T(512)S(1)}, f32[512]{0:T(512)}, u32[]{:S(2)}) copy-start(f32[512]{0:T(512)} %param.23) | copy-start | bytes 6148
  232.7 3.3 %copy-start.4 = (bf16[1024,512]{1,0:T(8,128)(2,1)S(1)}, bf16[1024,512]{1,0:T(8,128)(2,1)}, u32[]{:S(2)}) copy-start(bf16[1024,512]{1,0:T(8,128)(2,1)} %param.22) | copy-start | bytes 3145732
  232.7 4.0 %copy-start.5 = (bf16[512,256]{1,0:T(8,128)(2,1)S(1)}, bf16[512,256]{1,0:T(8,128)(2,1)}, u32[]{:S(2)}) copy-start(bf16[512,256]{1,0:T(8,128)(2,1)} %param.24) | copy-start | bytes 786436
  232.7 4.0 %copy-start.9 = (f32[256]{0:T(256)S(1)}, f32[256]{0:T(256)}, u32[]{:S(2)}) copy-start(f32[256]{0:T(256)} %param.25) | copy-start | bytes 3076
where the time goes:
time: 244 us; the launch traced here: 243 us
  waiting for transfers between devices  158 us (65%)
  local copies, waits for them, and re-layouts  39.8 us (16%)
  matrix products  17 us (7%)
  starting transfers between devices  13.3 us (5%)
  other arithmetic  8.71 us (4%)
  blocking collectives  5.2 us (2%)
    all_to_all x1, waiting for transfers between devices, per_device(): lax.all_to_all(packed_codes, 'tbl', split_axis=2, concat_axis=0, tiled=True)  158 us
    gather x2, local copies, waits for them, and re-layouts, scorer(): picked_codes = jnp.take(got_codes[:, :, 0, :], positions, axis=0)  18.8 us
    dot_general x2, matrix products, score_samples(): jnp.einsum('icb,jcb->bij', block_codes, block_codes, precision=lax.Precis...  12.6 us
    reshape x2, local copies, waits for them, and re-layouts, score_samples(): flat = gram.reshape(count, table_count * table_count)  9.12 us
    select_n x2, other arithmetic, scorer(): picked_codes = jnp.take(got_codes[:, :, 0, :], positions, axis=0)  7.4 us
    all_to_all x1, starting transfers between devices, per_device(): lax.all_to_all(packed_scales.astype(jnp.bfloat16), 'tbl', split_axis=2, c...  7.31 us
    reshape x1, local copies, waits for them, and re-layouts, per_device(): codes.reshape(slot_count, column_count, tbl_count, batch_local)  7.22 us
    all_to_all x1, starting transfers between devices, per_device(): lax.all_to_all(packed_codes, 'tbl', split_axis=2, concat_axis=0, tiled=True)  6.03 us
  transfers between devices with their start and end apart: 2, of which 2 were waited for; matrix products, arithmetic and copies ran while one was open for 4% of the time, Pallas kernels for 0%

commit v1 on v0

--- a/solution.py
+++ b/solution.py
@@ -3,6 +3,7 @@
 import numpy as np
 from jax import lax
 from jax.sharding import PartitionSpec as P
+from jax.lax import all_to_all, axis_size
 
 TABLES = 27
 
@@ -67,6 +68,13 @@
     weight_out,
     bias_out,
 ):
+
+    def _proceed_series_all(array_in):
+        val = axis_size("tbl")
+        now = jnp.split(array_in, val, axis=2)
+        block_out = all_to_all(jnp.stack(now), "tbl", 0, 0)
+        return jnp.concatenate(block_out, axis=0)
+
     layers = (
         (weight_first, bias_first),
         (weight_second, bias_second),
@@ -95,7 +103,7 @@
     scorer = make_scorer(shard_positions(shard_slot, shard_total))
     logits = scorer(
         (
-            lax.all_to_all(packed_codes, "tbl", split_axis=2, concat_axis=0, tiled=True),
+            _proceed_series_all(packed_codes),
             lax.all_to_all(
                 packed_scales.astype(jnp.bfloat16), "tbl", split_axis=2, concat_axis=0, tiled=True
             ).astype(packed_scales.dtype),

time: 244 us -> 271 us (1.11)
  local copies, waits for them, and re-layouts: 39.8 us -> 67.5 us
    unnamed x25 -> x39, local copies, waits for them, and re-layouts: 0.7 us -> 20.4 us
    split x0 -> x1, local copies, waits for them, and re-layouts: none -> 14 us  [_proceed_series_all(): now = jnp.split(array_in, val, axis=2)]
    reshape x1 -> x0, local copies, waits for them, and re-layouts: 7.22 us -> none  [per_device(): codes.reshape(slot_count, column_count, tbl_count, batch_local)]
  transfers between devices with their start and end apart: 2 -> 2, of which waited for: 2 -> 1; matrix products, arithmetic and copies ran while one was open for 4% -> 13% of each run, Pallas kernels for 0% -> 0%
where the time goes in v1:
time: 271 us
  waiting for transfers between devices  158 us (58%)
  local copies, waits for them, and re-layouts  67.5 us (25%)
  matrix products  17 us (6%)
  starting transfers between devices  13.5 us (5%)
  other arithmetic  8.71 us (3%)
  blocking collectives  5.2 us (2%)
    all_to_all x1, waiting for transfers between devices, _proceed_series_all(): block_out = all_to_all(jnp.stack(now), 'tbl', 0, 0)  158 us
    unnamed x39, local copies, waits for them, and re-layouts  20.4 us
    gather x2, local copies, waits for them, and re-layouts, scorer(): picked_codes = jnp.take(got_codes[:, :, 0, :], positions, axis=0)  18.7 us
    split x1, local copies, waits for them, and re-layouts, _proceed_series_all(): now = jnp.split(array_in, val, axis=2)  14 us
    dot_general x2, matrix products, score_samples(): jnp.einsum('icb,jcb->bij', block_codes, block_codes, precision=lax.Precis...  12.6 us
    reshape x2, local copies, waits for them, and re-layouts, score_samples(): flat = gram.reshape(count, table_count * table_count)  9.11 us
    select_n x2, other arithmetic, scorer(): picked_codes = jnp.take(got_codes[:, :, 0, :], positions, axis=0)  7.4 us
    all_to_all x1, starting transfers between devices, per_device(): lax.all_to_all(packed_scales.astype(jnp.bfloat16), 'tbl', split_axis=2, c...  7.31 us
  transfers between devices with their start and end apart: 2, of which 1 were waited for; matrix products, arithmetic and copies ran while one was open for 13% of the time, Pallas kernels for 0%

profile of v1, /device:TPU:0, one launch (start us, length us, event | category | flops | bytes accessed | tf_op | source)
XLA Modules:
  0.0 270.7 jit_solution(3295822728417463317)
XLA Ops:
  0.0 0.0 copy-start
  0.0 1.1 convert_element_type.56
  1.2 0.7 copy.117
  1.9 7.3 %all-to-all-start.1 = ((bf16[14,1,8,512]{3,0,1,2:T(8,128)(2,1)}), bf16[14,1,8,512]{3,0,1,2:T(8,128)(2,1)S(1)}, u32[]{:S(2)}, u32[]{:S(2)}) async-start(bf16[14,1,8,512]{3,0,1,2:T(8,128)(2,1)} %copy.117), calls=%async_computation.1 | async-start | bytes 262144 | tf_op jit(solution)/shard_map/all_to_all | solution.py:107
  9.2 8.0 %copy.130 = bf16[112,8,8,512]{3,2,1,0:T(8,128)(2,1)S(1)} copy(bf16[112,8,8,512]{3,1,2,0:T(8,128)(2,1)} %bitcast.74) | data formatting | bytes 14680064
  17.2 14.0 %fusion.8 = (bf16[14,64,1,512]{3,2,1,0:T(2,128)(2,1)S(1)}, bf16[14,64,1,512]{3,2,1,0:T(2,128)(2,1)S(1)}, bf16[14,64,1,512]{3,2,1,0:T(2,128)(2,1)}, bf16[14,64,1,...) fusion(bf16[14,64,8,512]{3,2,1,0:T(8,128)(2,1)S(1)} %bitcast.72), kind=kLoop, calls=%fused_computation.41 | loop fusion | bytes 14680064 | tf_op jit(solution)/shard_map/split | solution.py:74
  31.2 2.8 %bitcast_dynamic-update-slice_fusion.7 = bf16[8,14,64,1,512]{4,2,1,3,0:T(8,128)(2,1)} fusion(bf16[14,64,1,512]{3,2,1,0:T(2,128)(2,1)} %get-tuple-element.12), kind=kLoop, calls=%fused_computation.24 | loop fusion | bytes 1835008
  34.0 2.8 %bitcast_dynamic-update-slice_fusion.6 = bf16[8,14,64,1,512]{4,2,1,3,0:T(8,128)(2,1)} fusion(bf16[8,14,64,1,512]{4,2,1,3,0:T(8,128)(2,1)} %bitcast_dynamic-update-slice_fusion.7, bf16[14,64,1,512]{3,2,1,0:T(2,128)(2,1)} %get-tuple-element.11), kind=kLoop, calls=%fused_computation.23 | loop fusion | bytes 2752512
  36.8 1.2 bitcast_dynamic-update-slice_fusion.5
  38.0 0.0 copy-done.4
  38.0 1.2 bitcast_dynamic-update-slice_fusion.4
  39.2 0.0 copy-done.3
  39.2 1.2 bitcast_dynamic-update-slice_fusion.3
  40.4 0.0 copy-done.2
  40.4 1.2 bitcast_dynamic-update-slice_fusion.2
  41.7 1.2 bitcast_dynamic-update-slice_fusion.1
  42.9 1.2 bitcast_dynamic-update-slice_fusion
  44.1 0.0 all-to-all-done.1
  44.1 6.1 %all-to-all-start = ((bf16[8,14,64,1,512]{4,2,1,3,0:T(8,128)(2,1)}), bf16[8,14,64,1,512]{4,2,1,3,0:T(8,128)(2,1)}, u32[]{:S(2)}, u32[]{:S(2)}) async-start(bf16[8,14,64,1,512]{4,2,1,3,0:T(8,128)(2,1)} %bitcast_dynamic-update-slice_fusion), calls=%async_computation | async-start | bytes 14680064 | tf_op jit(solution)/shard_map/all_to_all | solution.py:75
  50.3 0.1 eq.15
  50.3 0.1 select_reduce_fusion
  50.4 0.1 reduce_sum.14
  50.6 0.1 copy.114
  50.7 0.0 copy-done.13
  51.5 0.6 gather_fusion.1
  52.1 0.1 gather.18
  52.2 0.2 copy.118
  52.5 157.9 %all-to-all-done = bf16[8,14,64,1,512]{4,2,1,3,0:T(8,128)(2,1)} async-done(((bf16[8,14,64,1,512]{4,2,1,3,0:T(8,128)(2,1)}), bf16[8,14,64,1,512]{4,2,1,3,0:T(8,128)(2,1)}, u32[]{:S(2)}, u32[]{:S(2)}) %all-to-all-start) | async-done | bytes 7340064 | tf_op jit(solution)/shard_map/all_to_all | solution.py:75
  210.4 5.7 %gather_fusion = bf16[54,64,512]{2,1,0:T(8,128)(2,1)} fusion(bf16[112,64,512]{2,1,0:T(8,128)(2,1)} %bitcast, s32[1024]{0:T(1024)S(1)} %pad_clamp_fusion.1), kind=kCustom, calls=%fused_computation | custom fusion | bytes 7078104 | tf_op jit(solution)/shard_map/jit(_take)/gather | solution.py:95
  216.1 13.1 %copy.115 = bf16[27,2,64,512]{2,0,3,1:T(8,128)(2,1)} copy(bf16[27,2,64,512]{3,2,1,0:T(8,128)(2,1)} %bitcast.73) | data formatting | bytes 7077888 | tf_op jit(solution)/shard_map/jit(_take)/gather | solution.py:95
  229.1 7.4 %broadcast_select_fusion = bf16[27,2,64,512]{2,0,3,1:T(8,128)(2,1)} fusion(bf16[27,2,64,512]{2,0,3,1:T(8,128)(2,1)} %copy.115, pred[27,2]{0,1:T(4,128)(4,1)S(1)} %copy.114), kind=kLoop, calls=%fused_computation.4 | loop fusion | flops 1769472 | bytes 7077942 | tf_op jit(solution)/shard_map/jit(_take)/select_n | solution.py:95
  236.5 5.9 %fusion = f32[512,27,27]{2,1,0:T(8,128)S(1)} fusion(bf16[27,2,64,512]{2,0,3,1:T(8,128)(2,1)} %broadcast_select_fusion), kind=kOutput, calls=%fused_computation.6 | convolution fusion | flops 47775744 | bytes 5687296 | tf_op jit(solution)/shard_map/icb,jcb->bij/dot_general | solution.py:39
  242.4 6.8 %multiply_add_fusion = bf16[512,27,27]{2,1,0:T(8,128)(2,1)} fusion(f32[512,27,27]{2,1,0:T(8,128)S(1)} %fusion, f32[512,27]{1,0:T(8,128)S(1)} %get-tuple-element.14, f32[512,27]{1,0:T(8,128)S(1)} %get-tuple-element.13, bf16[27,2,64,512]{2,0,3,1:T(8,128)(2,1)S(1)} %copy-done.1), kind=kOutput, calls=%fused_computation.3 | convolution fusion | flops 50015232 | bytes 14377984 | tf_op jit(solution)/shard_map/icb,jcb->bij/dot_general | solution.py:39
  249.2 7.7 %reshape.99 = bf16[512,729]{1,0:T(8,128)(2,1)} reshape(bf16[512,27,27]{2,1,0:T(8,128)(2,1)} %multiply_add_fusion) | data formatting | bytes 1492992 | tf_op jit(solution)/shard_map/reshape | solution.py:45
  256.9 1.4 copy.120
  258.3 0.0 copy-start.11
  258.3 2.0 gather_fusion.2
  260.4 0.0 copy-done.9
  260.4 0.0 copy-start.7
  260.4 0.0 copy-start.8
  260.4 0.0 copy-start.12
  260.4 1.9 maximum_convert_fusion.1
  262.4 1.3 maximum_convert_fusion
  263.7 0.7 fusion.3
  264.4 0.3 fusion.5
  264.7 0.2 fusion.9
  264.9 5.2 %all-gather.1 = f32[4,1,512]{2,1,0:T(1,128)S(1)} all-gather(f32[1,1,512]{2,1,0:T(1,128)S(1)} %bitcast.78), channel_id=2, replica_groups=mesh['tbl'=8,'pair'=4] {'pair'}, dimensions={0}, use_global_device_ids=true | all-gather | bytes 10240 | tf_op jit(solution)/shard_map/all_gather | solution.py:112
  270.1 0.6 copy.141
  (30 shorter events, 0.2 us)
Async XLA Ops:
  0.0 262.4 %copy-start = (bf16[1024,1024]{1,0:T(8,128)(2,1)S(1)}, bf16[1024,1024]{1,0:T(8,128)(2,1)}, u32[]{:S(2)}) copy-start(bf16[1024,1024]{1,0:T(8,128)(2,1)} %param.20) | copy-start | bytes 6291460
  1.9 42.2 %all-to-all-start.1 = ((bf16[14,1,8,512]{3,0,1,2:T(8,128)(2,1)}), bf16[14,1,8,512]{3,0,1,2:T(8,128)(2,1)S(1)}, u32[]{:S(2)}, u32[]{:S(2)}) async-start(bf16[14,1,8,512]{3,0,1,2:T(8,128)(2,1)} %copy.117), calls=%async_computation.1 | async-start | bytes 262144 | tf_op jit(solution)/shard_map/all_to_all | solution.py:107
  31.2 6.8 %copy-start.4 = (bf16[14,64,1,512]{3,2,1,0:T(2,128)(2,1)S(1)}, bf16[14,64,1,512]{3,2,1,0:T(2,128)(2,1)}, u32[]{:S(2)}) copy-start(bf16[14,64,1,512]{3,2,1,0:T(2,128)(2,1)} %get-tuple-element.9) | copy-start | bytes 2752516
  31.2 8.0 %copy-start.3 = (bf16[14,64,1,512]{3,2,1,0:T(2,128)(2,1)S(1)}, bf16[14,64,1,512]{3,2,1,0:T(2,128)(2,1)}, u32[]{:S(2)}) copy-start(bf16[14,64,1,512]{3,2,1,0:T(2,128)(2,1)} %get-tuple-element.8) | copy-start | bytes 2752516
  31.2 9.2 %copy-start.2 = (bf16[14,64,1,512]{3,2,1,0:T(2,128)(2,1)S(1)}, bf16[14,64,1,512]{3,2,1,0:T(2,128)(2,1)}, u32[]{:S(2)}) copy-start(bf16[14,64,1,512]{3,2,1,0:T(2,128)(2,1)} %get-tuple-element.7) | copy-start | bytes 2752516
  44.1 6.2 %copy-start.5 = (s32[8,14]{1,0:T(8,128)S(1)}, s32[8,14]{1,0:T(8,128)}, u32[]{:S(2)}) copy-start(s32[8,14]{1,0:T(8,128)} %param.17) | copy-start | bytes 1348
  44.1 6.6 %copy-start.13 = (bf16[256]{0:T(256)(128)(2,1)S(1)}, bf16[256]{0:T(256)(128)(2,1)}, u32[]{:S(2)}) copy-start(bf16[256]{0:T(256)(128)(2,1)} %param.26) | copy-start | bytes 1540
  44.1 7.3 %copy-start.6 = (s32[351]{0:T(512)S(1)}, s32[351]{0:T(512)}, u32[]{:S(2)}) copy-start(s32[351]{0:T(512)} %constant.49) | copy-start | bytes 4216
  44.1 166.3 %all-to-all-start = ((bf16[8,14,64,1,512]{4,2,1,3,0:T(8,128)(2,1)}), bf16[8,14,64,1,512]{4,2,1,3,0:T(8,128)(2,1)}, u32[]{:S(2)}, u32[]{:S(2)}) async-start(bf16[8,14,64,1,512]{4,2,1,3,0:T(8,128)(2,1)} %bitcast_dynamic-update-slice_fusion), calls=%async_computation | async-start | bytes 14680064 | tf_op jit(solution)/shard_map/all_to_all | solution.py:75
  236.5 5.9 %copy-start.1 = (bf16[27,2,64,512]{2,0,3,1:T(8,128)(2,1)S(1)}, bf16[27,2,64,512]{2,0,3,1:T(8,128)(2,1)}, u32[]{:S(2)}) copy-start(bf16[27,2,64,512]{2,0,3,1:T(8,128)(2,1)} %broadcast_select_fusion) | copy-start | bytes 10616836
  249.2 11.2 %copy-start.9 = (f32[1024]{0:T(1024)S(1)}, f32[1024]{0:T(1024)}, u32[]{:S(2)}) copy-start(f32[1024]{0:T(1024)} %param.19) | copy-start | bytes 12292
  249.2 13.2 %copy-start.10 = (f32[1024]{0:T(1024)S(1)}, f32[1024]{0:T(1024)}, u32[]{:S(2)}) copy-start(f32[1024]{0:T(1024)} %param.21) | copy-start | bytes 12292
  258.3 5.4 %copy-start.11 = (f32[512]{0:T(512)S(1)}, f32[512]{0:T(512)}, u32[]{:S(2)}) copy-start(f32[512]{0:T(512)} %param.23) | copy-start | bytes 6148
  260.4 3.3 %copy-start.7 = (bf16[1024,512]{1,0:T(8,128)(2,1)S(1)}, bf16[1024,512]{1,0:T(8,128)(2,1)}, u32[]{:S(2)}) copy-start(bf16[1024,512]{1,0:T(8,128)(2,1)} %param.22) | copy-start | bytes 3145732
  260.4 4.0 %copy-start.8 = (bf16[512,256]{1,0:T(8,128)(2,1)S(1)}, bf16[512,256]{1,0:T(8,128)(2,1)}, u32[]{:S(2)}) copy-start(bf16[512,256]{1,0:T(8,128)(2,1)} %param.24) | copy-start | bytes 786436
  260.4 4.0 %copy-start.12 = (f32[256]{0:T(256)S(1)}, f32[256]{0:T(256)}, u32[]{:S(2)}) copy-start(f32[256]{0:T(256)} %param.25) | copy-start | bytes 3076
